TPU v7x, 256 devices: a whole 4x4x8 slice. The times are simulated.
256 devices in a mesh: ctx: 16 (over y, x), tp: 8 (over z), dp: 2 (over core).
Axes of the slice: x: 4, y: 4, z: 8, core: 2. Of those that a mesh axis runs over, the one named last changes fastest.
Arguments:
- query_latent: bfloat16 [2, 2048, 32768], P('dp', 'ctx', 'tp'), may hold values from -120 to 120
- query_rotary: bfloat16 [2, 2048, 4096], P('dp', 'ctx', 'tp'), may hold values from -6 to 6
- key_latent: bfloat16 [2, 2048, 512], P('dp', 'ctx'), may hold values from -6 to 6
- key_rotary: bfloat16 [2, 2048, 64], P('dp', 'ctx'), may hold values from -6 to 6
- value_up: bfloat16 [64, 512, 128], P('tp', 'ctx'), may hold values from -0.25 to 0.25
- out_proj: bfloat16 [64, 128, 3584], P('tp', None, 'ctx'), may hold values from -0.0625 to 0.0625
- residual: bfloat16 [2, 2048, 3584], P('dp', ('ctx', 'tp')), may hold values from -0.59765625 to 0.59765625
- norm_gain: float32 [3584], replicated, may hold values from 0.1 to 1.9
- gate_proj: bfloat16 [128, 3584, 1024], P(('ctx', 'tp'), 'dp'), may hold values from -0.09375 to 0.09375
- up_proj: bfloat16 [128, 3584, 1024], P(('ctx', 'tp'), 'dp'), may hold values from -0.09375 to 0.09375
- down_proj: bfloat16 [128, 1024, 3584], P(('ctx', 'tp'), 'dp'), may hold values from -0.1875 to 0.1875
- expert_ids: int32 [2, 2048, 8], P('dp', ('ctx', 'tp')), may hold values from 0 to 127, all different within a row; in each aligned block of 16 rows (0 to 15, 16 to 31, ..., all dimensions but the last counted through in order) at most 2 rows name the same one
- route_score: float32 [2, 2048, 8], P('dp', ('ctx', 'tp')), may hold values from 0.05 to 1
- out_grad: bfloat16 [2, 2048, 3584], P('dp', ('ctx', 'tp')), may hold values from -6 to 6
Outputs:
- layer_out: bfloat16 [2, 2048, 3584], P('dp', ('ctx', 'tp'))
- resid_grad: bfloat16 [2, 2048, 3584], P('dp', ('ctx', 'tp'))
- score_grad: float32 [2, 2048, 8], P('dp', ('ctx', 'tp'))
Inputs may be any that keep to these rules, and one draw needn't show every extreme that they name: `expert_ids`: each token names 8 different experts. In each aligned block of 16 tokens of one sequence no expert is named by more than 2 tokens, a bound that some block reaches.
All inputs are finite; a program needn't handle non-finite values.
Results may differ from a plain program's by a relative error of at most 0.034.
Values may be sent and summed in bfloat16 or wider, within the bound.
A program may use at most 128 MiB of HBM per device.

v0:
```python
import jax
import jax.numpy as jnp
from jax import lax
from jax.sharding import PartitionSpec as P

route_scale = 2.5
norm_eps = 1e-06


def rms_scale(rows_in, norm_gain):
    inverse = lax.rsqrt(jnp.mean(rows_in * rows_in, axis=-1, keepdims=True) + norm_eps)
    return rows_in * inverse * norm_gain


def expert_pass(rows_u, rows_g, gate_w, up_w, down_w):
    act_a = jnp.dot(rows_u, gate_w, preferred_element_type=jnp.float32)
    act_b = jnp.dot(rows_u, up_w, preferred_element_type=jnp.float32)
    gated_act = jax.nn.silu(act_a)
    hidden = (gated_act * act_b).astype(jnp.bfloat16)
    result = jnp.dot(hidden, down_w, preferred_element_type=jnp.float32).astype(jnp.bfloat16)
    d_hidden = jnp.dot(rows_g, down_w.T, preferred_element_type=jnp.float32)
    sigmoid_a = jax.nn.sigmoid(act_a)
    slope_a = sigmoid_a * (1.0 + act_a * (1.0 - sigmoid_a))
    d_gate = (d_hidden * act_b * slope_a).astype(jnp.bfloat16)
    d_up = (d_hidden * gated_act).astype(jnp.bfloat16)
    d_rows = jnp.dot(d_gate, gate_w.T, preferred_element_type=jnp.float32) + jnp.dot(
        d_up, up_w.T, preferred_element_type=jnp.float32
    )
    return (result, d_rows.astype(jnp.bfloat16))


def head_outputs(latent_out, value_maps):
    rows_here, head_count = (latent_out.shape[1], latent_out.shape[0])
    mapped = jnp.einsum("hqc,hcv->qhv", latent_out, value_maps, preferred_element_type=jnp.float32)
    return mapped.astype(jnp.bfloat16).reshape(rows_here, head_count * value_maps.shape[2])


def per_device(
    query_latent,
    query_rotary,
    key_latent,
    key_rotary,
    value_up,
    out_proj,
    residual,
    norm_gain,
    gate_proj,
    up_proj,
    down_proj,
    expert_ids,
    route_score,
    out_grad,
):
    ctx_count = lax.axis_size("ctx")
    tp_count = lax.axis_size("tp")
    ctx_index = lax.axis_index("ctx")
    rows_here = query_latent.shape[1]
    head_count = value_up.shape[0]
    latent_width = key_latent.shape[2]
    rope_width = key_rotary.shape[2]
    value_width = value_up.shape[2]
    model_width = residual.shape[2]
    scale = (value_width + rope_width) ** (-0.5)
    queries = query_latent[0].reshape(rows_here, head_count, latent_width)
    rotary = query_rotary[0].reshape(rows_here, head_count, rope_width)
    query_pos = ctx_index * rows_here + jnp.arange(rows_here, dtype=jnp.int32)
    last_query = ctx_index * rows_here + rows_here - 1
    initial = (
        jnp.full((head_count, rows_here), -1e30, jnp.float32),
        jnp.zeros((head_count, rows_here), jnp.float32),
        jnp.zeros((head_count, rows_here, latent_width), jnp.float32),
    )
    pieces = (
        lax.all_gather(key_latent, "ctx", axis=1, tiled=True),
        lax.all_gather(key_rotary, "ctx", axis=1, tiled=True),
    )

    def compute(running):
        row_top, row_total, weighted = running
        key_block = pieces[0][0]
        rot_block = pieces[1][0]
        key_count = key_block.shape[0]
        scores = jnp.einsum("qhc,kc->hqk", queries, key_block, preferred_element_type=jnp.float32)
        scores = scores + jnp.einsum(
            "qhr,kr->hqk", rotary, rot_block, preferred_element_type=jnp.float32
        )
        key_pos = jnp.arange(key_count, dtype=jnp.int32)
        causal = key_pos[None, None, :] <= query_pos[None, :, None]
        scores = jnp.where(causal, scores * scale, -1e30)
        new_top = jnp.maximum(row_top, jnp.max(scores, axis=2))
        exp_terms = jnp.where(causal, jnp.exp(scores - new_top[:, :, None]), 0.0)
        row_total = jnp.sum(exp_terms, axis=2)
        weighted = jnp.einsum(
            "hqk,kc->hqc",
            exp_terms.astype(jnp.bfloat16),
            key_block,
            preferred_element_type=jnp.float32,
        )
        return (new_top, row_total, weighted)

    row_top, row_total, weighted = lax.cond(
        jnp.int32(0) <= last_query, compute, lambda running: running, initial
    )
    latent_out = (weighted / row_total[:, :, None]).astype(jnp.bfloat16)
    tok_rows = rows_here // tp_count
    value_maps, out_maps = (
        lax.all_gather(value_up, "ctx", axis=1, tiled=True),
        lax.all_gather(out_proj, "ctx", axis=2, tiled=True),
    )
    heads_out = head_outputs(latent_out, value_maps)
    flat_out = out_maps.reshape(head_count * value_width, model_width)
    attn_rows = lax.psum_scatter(
        jnp.dot(heads_out, flat_out, preferred_element_type=jnp.float32).astype(jnp.bfloat16),
        "tp",
        scatter_dimension=0,
        tiled=True,
    ).astype(jnp.float32)
    hidden_sum = residual[0].astype(jnp.float32) + attn_rows
    normed = rms_scale(hidden_sum, norm_gain).astype(jnp.bfloat16)
    route_ids = expert_ids[0]
    top_count = route_ids.shape[1]
    experts = ctx_count * tp_count
    capacity = 2 * tok_rows * top_count // experts
    flat_ids = route_ids.reshape(tok_rows * top_count)
    chosen = (flat_ids[:, None] == jnp.arange(experts, dtype=jnp.int32)[None, :]).astype(jnp.int32)
    earlier = jnp.cumsum(chosen, axis=0) - chosen
    slot_index = jnp.sum(earlier * chosen, axis=1)
    target = flat_ids * capacity + slot_index
    select = (target[:, None] == jnp.arange(experts * capacity, dtype=jnp.int32)[None, :]).astype(
        jnp.bfloat16
    )
    placing = jnp.sum(select.reshape(tok_rows, top_count, experts * capacity), axis=1)
    paired = jnp.concatenate([normed, out_grad[0]], axis=1)
    outgoing = jnp.dot(placing.T, paired, preferred_element_type=jnp.float32).astype(jnp.bfloat16)
    outgoing = outgoing.reshape(experts, capacity, 2, model_width)
    gate_full, up_full, down_full = (
        lax.all_gather(gate_proj, "dp", axis=1, tiled=True),
        lax.all_gather(up_proj, "dp", axis=1, tiled=True),
        lax.all_gather(down_proj, "dp", axis=1, tiled=True),
    )
    gate_w = gate_full[0]
    up_w = up_full[0]
    down_w = down_full[0]
    arrived = lax.all_to_all(outgoing, ("ctx", "tp"), split_axis=0, concat_axis=0, tiled=True)
    sources = arrived.shape[0]
    slot_count = arrived.shape[1]
    slot_rows = arrived.reshape(sources * slot_count, 2, model_width)
    result, d_rows = expert_pass(slot_rows[:, 0], slot_rows[:, 1], gate_w, up_w, down_w)
    going_back = jnp.stack([result, d_rows], axis=1).reshape(sources, slot_count, 2, model_width)
    returned = lax.all_to_all(going_back, ("ctx", "tp"), split_axis=0, concat_axis=0, tiled=True)
    per_route = jnp.dot(
        select,
        returned.reshape(experts * capacity, 2 * model_width),
        preferred_element_type=jnp.float32,
    )
    per_route = per_route.reshape(tok_rows, top_count, 2, model_width)
    route_out = per_route[:, :, 0]
    route_grad = per_route[:, :, 1]
    route_raw = route_score[0]
    score_total = jnp.sum(route_raw, axis=1, keepdims=True)
    route_weight = route_scale * route_raw / score_total
    mixed_out = hidden_sum + jnp.einsum(
        "tk,tkd->td", route_weight, route_out, precision=lax.Precision.HIGHEST
    )
    grad_rows = out_grad[0].astype(jnp.float32)
    weight_grad = jnp.einsum("td,tkd->tk", grad_rows, route_out, precision=lax.Precision.HIGHEST)
    d_normed = jnp.einsum("tk,tkd->td", route_weight, route_grad, precision=lax.Precision.HIGHEST)
    unused, pullback = jax.vjp(lambda rows_in: rms_scale(rows_in, norm_gain), hidden_sum)
    resid_grad = (grad_rows + pullback(d_normed)[0]).astype(jnp.bfloat16)
    score_grad = (
        route_scale
        / score_total
        * (weight_grad - jnp.sum(weight_grad * route_raw, axis=1, keepdims=True) / score_total)
    )
    return (mixed_out.astype(jnp.bfloat16)[None], resid_grad[None], score_grad[None])


def solution(mesh):
    return jax.shard_map(
        per_device,
        mesh=mesh,
        in_specs=(
            P("dp", "ctx", "tp"),
            P("dp", "ctx", "tp"),
            P("dp", "ctx", None),
            P("dp", "ctx", None),
            P("tp", "ctx", None),
            P("tp", None, "ctx"),
            P("dp", ("ctx", "tp"), None),
            P(),
            P(("ctx", "tp"), "dp", None),
            P(("ctx", "tp"), "dp", None),
            P(("ctx", "tp"), "dp", None),
            P("dp", ("ctx", "tp"), None),
            P("dp", ("ctx", "tp"), None),
            P("dp", ("ctx", "tp"), None),
        ),
        out_specs=(
            P("dp", ("ctx", "tp"), None),
            P("dp", ("ctx", "tp"), None),
            P("dp", ("ctx", "tp"), None),
        ),
        check_vma=False,
    )
```

profile of v0, /device:TPU:32, one launch (start us, length us, event | category | flops | bytes accessed | tf_op | source)
XLA Modules:
  0.0 521.7 jit_solution(13411717028966328108)
XLA Ops:
  8.0 0.7 all-gather.7.cloned.1.call-update
  8.8 0.7 all-gather.9.cloned.1.call-update
  9.5 0.7 all-gather.11.cloned.1.call-update
  10.3 24.5 %all_gather.22 = bf16[1,2048,64]{1,2,0:T(8,128)(2,1)S(1)} all-gather(bf16[1,128,64]{1,2,0:T(8,128)(2,1)} %param.19), channel_id=1, replica_groups=mesh['ctx'=16,'tp'=8,'dp'=2] {'ctx'}, dimensions={1}, use_global_device_ids=true | all-gather | bytes 278528 | tf_op jit(solution)/shard_map/all_gather | solution.py:75
  34.7 29.1 %all-gather.7.cloned.1.call-done = bf16[1,2048,512]{2,1,0:T(8,128)(2,1)} async-done(((bf16[1,128,512]{2,1,0:T(8,128)(2,1)}), bf16[1,2048,512]{2,1,0:T(8,128)(2,1)}) %all-gather.7.cloned.1.call-update) | async-done | bytes 2097168 | tf_op jit(solution)/shard_map/all_gather | solution.py:74
  63.8 17.5 %conditional.1 = (f32[8,128]{1,0:T(8,128)S(1)}, f32[8,128,512]{2,1,0:T(8,128)S(1)}) conditional(s32[]{:T(128)} %convert_element_type.68, () %tuple.16, (s32[]{:T(128)}, s32[128]{0:T(128)S(1)}, bf16[1,2048,512]{2,1,0:T(8,128)(2,1)}, bf16[1,128,4096]{2,1,0:T(8,128)(2,1)}, bf16[1,2048,64]{1,2,0:T(8,128)(2,1)S(1)}, ...), branch_computations={%region_0.0_spmd, %region_1.4_spmd} | conditional | flops 4584635392 | bytes 62023244 | solution.py:101
  63.9 0.2 iota_compare_fusion
  64.0 1.6 copy.58
  65.7 6.4 %fusion.8 = f32[2048,128,8]{1,0,2:T(8,128)} fusion(bf16[1,2048,512]{2,1,0:T(8,128)(2,1)} %get-tuple-element.18, bf16[128,8,512]{2,1,0:T(8,128)(2,1)S(1)} %bitcast.136), kind=kOutput, calls=%fused_computation.9 | convolution fusion | flops 2147483648 | bytes 11534336 | tf_op jit(solution)/shard_map/cond/branch_1_fun/qhc,kc->hqk/dot_general | solution.py:83
  72.2 5.2 fusion.69
  77.4 2.4 fusion.2
  79.9 1.4 fusion.1
  81.3 32.7 %all-gather.9.cloned.1.call-done = bf16[8,512,128]{2,1,0:T(8,128)(2,1)} async-done(((bf16[8,32,128]{2,1,0:T(8,128)(2,1)}), bf16[8,512,128]{2,1,0:T(8,128)(2,1)}) %all-gather.9.cloned.1.call-update) | async-done | bytes 1048592 | tf_op jit(solution)/shard_map/all_gather | solution.py:107
  114.0 73.1 %all-gather.11.cloned.1.call-done = bf16[8,128,3584]{1,2,0:T(8,128)(2,1)} async-done(((bf16[8,128,224]{1,2,0:T(8,128)(2,1)}), bf16[8,128,3584]{1,2,0:T(8,128)(2,1)}) %all-gather.11.cloned.1.call-update) | async-done | bytes 7340048 | tf_op jit(solution)/shard_map/all_gather | solution.py:108
  187.1 7.2 %fusion.34 = bf16[128,3584]{1,0:T(8,128)(2,1)} fusion(bf16[8,128,3584]{1,2,0:T(8,128)(2,1)} %all-gather.11.cloned.1.call-done, bf16[8,512,128]{2,1,0:T(8,128)(2,1)} %all-gather.9.cloned.1.call-done, f32[8,128,512]{2,1,0:T(8,128)S(1)} %get-tuple-element.27, f32[8,128]{1,0:T(8,128)S(1)} %get-tuple-element.28), kind=kOutput, calls=%fused_computation.34 | convolution fusion | flops 1075380224 | bytes 11407360 | tf_op jit(solution)/shard_map/dot_general | solution.py:113
  194.5 0.5 all-gather.13.cloned.1.call-update
  195.0 11.6 %all-gather.15.cloned.1.call-start = ((), (), s32[]{:S(2)}) async-start(), calls=%async_computation.8 | async-start | bytes 11010048 | tf_op jit(solution)/shard_map/all_gather | solution.py:138
  206.9 0.2 reduce_window_sum.11
  207.6 24.1 %reduce-scatter.2.cloned.1.call-done = bf16[16,3584]{1,0:T(8,128)(2,1)} async-done(((bf16[128,3584]{1,0:T(8,128)(2,1)}), bf16[16,3584]{1,0:T(8,128)(2,1)}) %reduce-scatter.2.cloned.1.call-update) | async-done | bytes 114704 | tf_op jit(solution)/shard_map/reduce_scatter | solution.py:112
  231.7 1.0 multiply_reduce_fusion.1
  232.8 1.0 multiply_convert_fusion.6
  233.8 3.0 convolution_convert_fusion
  236.8 9.5 %reshape.124 = bf16[128,2,2,3584]{3,2,1,0:T(2,128)(2,1)} reshape(bf16[256,7168]{1,0:T(8,128)(2,1)} %convolution_convert_fusion) | data formatting | bytes 7340032 | tf_op jit(solution)/shard_map/reshape | solution.py:135
  246.3 12.2 %all-to-all-start = ((bf16[128,2,2,3584]{3,2,1,0:T(2,128)(2,1)}), bf16[128,2,2,3584]{3,2,1,0:T(2,128)(2,1)}, u32[]{:S(2)}, u32[]{:S(2)}) async-start(bf16[128,2,2,3584]{3,2,1,0:T(2,128)(2,1)} %reshape.124), calls=%async_computation.1 | async-start | bytes 7340032 | tf_op jit(solution)/shard_map/all_to_all | solution.py:144
  258.5 0.5 all-gather.17.cloned.1.call-update
  259.0 82.3 %all-to-all-done = bf16[128,2,2,3584]{3,2,1,0:T(2,128)(2,1)} async-done(((bf16[128,2,2,3584]{3,2,1,0:T(2,128)(2,1)}), bf16[128,2,2,3584]{3,2,1,0:T(2,128)(2,1)}, u32[]{:S(2)}, u32[]{:S(2)}) %all-to-all-start) | async-done | bytes 3670048 | tf_op jit(solution)/shard_map/all_to_all | solution.py:144
  341.3 8.9 %fusion.70 = (bf16[256,1,3584]{2,1,0:T(2,128)(2,1)}, bf16[256,1,3584]{2,1,0:T(2,128)(2,1)}) fusion(bf16[256,2,3584]{2,1,0:T(2,128)(2,1)} %bitcast.16), kind=kLoop, calls=%fused_computation.96 | loop fusion | bytes 7340032 | tf_op jit(solution)/shard_map/slice | solution.py:148
  350.2 6.3 %fusion.23 = f32[256,1024]{1,0:T(8,128)S(1)} fusion(bf16[1,3584,1024]{2,1,0:T(8,128)(2,1)} %all-gather.13.cloned.1.call-done, bf16[256,1,3584]{2,1,0:T(2,128)(2,1)} %get-tuple-element.53), kind=kOutput, calls=%fused_computation.28 | convolution fusion | flops 1879048192 | bytes 10223616 | tf_op jit(solution)/shard_map/dot_general | solution.py:16
  356.5 7.3 %fusion.19 = f32[256,1024]{1,0:T(8,128)} fusion(bf16[1,3584,1024]{2,1,0:T(8,128)(2,1)} %all-gather.15.cloned.1.call-done, bf16[256,1,3584]{2,1,0:T(2,128)(2,1)} %get-tuple-element.53), kind=kOutput, calls=%fused_computation.24 | convolution fusion | flops 1879048192 | bytes 10223616 | tf_op jit(solution)/shard_map/dot_general | solution.py:17
  363.8 6.4 %fusion.13 = f32[256,1024]{1,0:T(8,128)S(1)} fusion(bf16[1,1024,3584]{2,1,0:T(8,128)(2,1)} %all-gather.17.cloned.1.call-done, bf16[256,1,3584]{2,1,0:T(2,128)(2,1)} %get-tuple-element.54), kind=kOutput, calls=%fused_computation.18 | convolution fusion | flops 1879048192 | bytes 10223616 | tf_op jit(solution)/shard_map/dot_general | solution.py:21
  370.2 1.0 copy-done.10
  371.2 2.2 fusion.17
  373.4 3.9 fusion.31
  377.3 3.7 stack.13
  381.0 5.5 %fusion.28 = bf16[256,3584]{1,0:T(8,128)(2,1)S(1)} fusion(bf16[1,1024,3584]{2,1,0:T(8,128)(2,1)} %all-gather.17.cloned.1.call-done, f32[256,1024]{1,0:T(8,128)} %fusion.19, f32[256,1024]{1,0:T(8,128)S(1)} %fusion.23), kind=kOutput, calls=%fused_computation.31 | convolution fusion | flops 1881538560 | bytes 11272192 | tf_op jit(solution)/shard_map/dot_general | solution.py:20
  386.5 3.8 stack.12
  390.3 9.8 %pad_maximum_fusion = bf16[128,2,2,3584]{3,2,1,0:T(2,128)(2,1)} fusion(bf16[128,2,1,3584]{3,2,1,0:T(2,128)(2,1)} %stack.13, bf16[128,2,1,3584]{3,2,1,0:T(2,128)(2,1)} %stack.12), kind=kLoop, calls=%fused_computation.35 | loop fusion | flops 7340032 | bytes 7340032 | tf_op jit(solution)/shard_map/stack | solution.py:149
  400.1 7.8 %all-to-all-start.1 = ((bf16[128,2,2,3584]{3,2,1,0:T(2,128)(2,1)}), bf16[128,2,2,3584]{3,2,1,0:T(2,128)(2,1)}, u32[]{:S(2)}, u32[]{:S(2)}) async-start(bf16[128,2,2,3584]{3,2,1,0:T(2,128)(2,1)} %pad_maximum_fusion), calls=%async_computation.2 | async-start | bytes 7340032 | tf_op jit(solution)/shard_map/all_to_all | solution.py:150
  408.0 80.6 %all-to-all-done.1 = bf16[128,2,2,3584]{3,2,1,0:T(2,128)(2,1)} async-done(((bf16[128,2,2,3584]{3,2,1,0:T(2,128)(2,1)}), bf16[128,2,2,3584]{3,2,1,0:T(2,128)(2,1)}, u32[]{:S(2)}, u32[]{:S(2)}) %all-to-all-start.1) | async-done | bytes 3670048 | tf_op jit(solution)/shard_map/all_to_all | solution.py:150
  488.6 4.4 copy.59
  493.0 5.9 %copy.47 = bf16[7168,256]{1,0:T(8,128)(2,1)} copy(bf16[7168,256]{0,1:T(8,128)(2,1)} %bitcast.133) | data formatting | bytes 7340032 | tf_op jit(solution)/shard_map/dot_general | solution.py:151
  499.0 3.4 fusion.51
  502.4 1.8 copy-done
  504.1 1.9 fusion.36
  506.2 3.1 fusion.37
  509.3 3.1 fusion.35
  512.6 0.6 fusion.61
  513.2 0.8 fusion.55
  (57 shorter events, 1.7 us)
Async XLA Ops:
  8.0 55.8 %all-gather.7.cloned.1.call-start = ((), (), s32[]{:S(2)}) async-start(), calls=%async_computation.3 | async-start | bytes 2228224 | tf_op jit(solution)/shard_map/all_gather | solution.py:74
  8.7 105.3 %all-gather.9.cloned.1.call-start = ((), (), s32[]{:S(2)}) async-start(), calls=%async_computation.4 | async-start | bytes 1114112 | tf_op jit(solution)/shard_map/all_gather | solution.py:107
  9.5 177.6 %all-gather.11.cloned.1.call-start = ((), (), s32[]{:S(2)}) async-start(), calls=%async_computation.5 | async-start | bytes 7798784 | tf_op jit(solution)/shard_map/all_gather | solution.py:108
  10.2 221.5 %reduce-scatter.2.cloned.1.call-start = ((), (), s32[]{:S(2)}) async-start(), calls=%async_computation.6 | async-start | bytes 1032192 | tf_op jit(solution)/shard_map/reduce_scatter | solution.py:112
  65.7 6.4 %copy-start.5 = (bf16[1,128,512]{2,1,0:T(8,128)(2,1)S(1)}, bf16[1,128,512]{2,1,0:T(8,128)(2,1)}, u32[]{:S(2)}) copy-start(bf16[1,128,512]{2,1,0:T(8,128)(2,1)} %get-tuple-element.50) | copy-start | bytes 393220 | tf_op jit(solution)/shard_map/cond
  72.2 5.2 %copy-start.9 = (bf16[1,2048,512]{2,1,0:T(8,128)(2,1)S(1)}, bf16[1,2048,512]{2,1,0:T(8,128)(2,1)}, u32[]{:S(2)}) copy-start(bf16[1,2048,512]{2,1,0:T(8,128)(2,1)} %get-tuple-element.18) | copy-start | bytes 6291460 | tf_op jit(solution)/shard_map/cond
  194.4 12.3 %copy-start.6 = (s32[1,16,8]{1,2,0:T(8,128)S(1)}, s32[1,16,8]{1,2,0:T(8,128)}, u32[]{:S(2)}) copy-start(s32[1,16,8]{1,2,0:T(8,128)} %param.27) | copy-start | bytes 1540
  194.4 37.4 %copy-start.1 = (bf16[1,16,3584]{2,1,0:T(8,128)(2,1)S(1)}, bf16[1,16,3584]{2,1,0:T(8,128)(2,1)}, u32[]{:S(2)}) copy-start(bf16[1,16,3584]{2,1,0:T(8,128)(2,1)} %param.22) | copy-start | bytes 344068
  194.4 38.4 %copy-start.4 = (f32[3584]{0:T(1024)S(1)}, f32[3584]{0:T(1024)}, u32[]{:S(2)}) copy-start(f32[3584]{0:T(1024)} %param.23) | copy-start | bytes 43012
  194.4 39.4 %copy-start.3 = (bf16[1,16,3584]{2,1,0:T(8,128)(2,1)S(1)}, bf16[1,16,3584]{2,1,0:T(8,128)(2,1)}, u32[]{:S(2)}) copy-start(bf16[1,16,3584]{2,1,0:T(8,128)(2,1)} %param.29) | copy-start | bytes 344068
  194.4 155.8 %all-gather.13.cloned.1.call-start = ((), (), s32[]{:S(2)}) async-start(), calls=%async_computation.7 | async-start | bytes 11010048 | tf_op jit(solution)/shard_map/all_gather | solution.py:137
  195.0 161.5 %all-gather.15.cloned.1.call-start = ((), (), s32[]{:S(2)}) async-start(), calls=%async_computation.8 | async-start | bytes 11010048 | tf_op jit(solution)/shard_map/all_gather | solution.py:138
  246.3 95.0 %all-to-all-start = ((bf16[128,2,2,3584]{3,2,1,0:T(2,128)(2,1)}), bf16[128,2,2,3584]{3,2,1,0:T(2,128)(2,1)}, u32[]{:S(2)}, u32[]{:S(2)}) async-start(bf16[128,2,2,3584]{3,2,1,0:T(2,128)(2,1)} %reshape.124), calls=%async_computation.1 | async-start | bytes 7340032 | tf_op jit(solution)/shard_map/all_to_all | solution.py:144
  258.4 105.3 %all-gather.17.cloned.1.call-start = ((), (), s32[]{:S(2)}) async-start(), calls=%async_computation.9 | async-start | bytes 11010048 | tf_op jit(solution)/shard_map/all_gather | solution.py:139
  363.8 7.4 %copy-start.8 = (bf16[1,3584,1024]{2,1,0:T(8,128)(2,1)S(1)}, bf16[1,3584,1024]{2,1,0:T(8,128)(2,1)}, u32[]{:S(2)}) copy-start(bf16[1,3584,1024]{2,1,0:T(8,128)(2,1)} %all-gather.15.cloned.1.call-done) | copy-start | bytes 22020100
  363.8 9.6 %slice-start = ((s8[7340032]{0:T(1024)(128)(4,1)}), s8[4194304]{0:T(1024)(128)(4,1)S(1)}, s32[]{:S(2)}) async-start(s8[7340032]{0:T(1024)(128)(4,1)} %bitcast.140), calls=%async_computation.10 | async-start | bytes 8388608
  370.2 1.0 copy-start.10
  371.2 2.2 slice-start.1
  400.1 7.8 %copy-start.7 = (f32[1,16,8]{1,2,0:T(8,128)S(1)}, f32[1,16,8]{1,2,0:T(8,128)}, u32[]{:S(2)}) copy-start(f32[1,16,8]{1,2,0:T(8,128)} %param.28) | copy-start | bytes 1540
  400.1 88.5 %all-to-all-start.1 = ((bf16[128,2,2,3584]{3,2,1,0:T(2,128)(2,1)}), bf16[128,2,2,3584]{3,2,1,0:T(2,128)(2,1)}, u32[]{:S(2)}, u32[]{:S(2)}) async-start(bf16[128,2,2,3584]{3,2,1,0:T(2,128)(2,1)} %pad_maximum_fusion), calls=%async_computation.2 | async-start | bytes 7340032 | tf_op jit(solution)/shard_map/all_to_all | solution.py:150
  502.3 1.8 copy-start
  502.3 10.1 %copy-start.2 = (bf16[16,3584]{1,0:T(8,128)(2,1)S(1)}, bf16[16,3584]{1,0:T(8,128)(2,1)}, u32[]{:S(2)}) copy-start(bf16[16,3584]{1,0:T(8,128)(2,1)} %reduce-scatter.2.cloned.1.call-done) | copy-start | bytes 344068
Sparse Core Ops, SparseCore 0:
  11.3 52.5 all-gather.6
  66.2 47.7 all-gather.8
  116.5 70.5 all-gather.10
  194.5 37.1 reduce-scatter.1
Sparse Core Ops, SparseCore 1:
  196.8 23.3 all-gather.12
  221.9 24.8 all-gather.14
  260.8 24.9 all-gather.16
where the time goes:
time: 530 us; the launch traced here: 522 us
  waiting for transfers between devices  325 us (61%)
  matrix products  67.2 us (13%)
  local copies, waits for them, and re-layouts  41.3 us (8%)
  starting transfers between devices  31.9 us (6%)
  blocking collectives  24.5 us (5%)
  between operations  16.1 us (3%)
  other arithmetic  15.6 us (3%)
    all_to_all x1, waiting for transfers between devices, per_device(): lax.all_to_all(outgoing, ('ctx', 'tp'), split_axis=0, concat_axis=0, tile...  82.3 us
    all_to_all x1, waiting for transfers between devices, per_device(): lax.all_to_all(going_back, ('ctx', 'tp'), split_axis=0, concat_axis=0, ti...  80.6 us
    all_gather x1, waiting for transfers between devices, per_device(): lax.all_gather(out_proj, 'ctx', axis=2, tiled=True)  73.1 us
    all_gather x1, waiting for transfers between devices, per_device(): lax.all_gather(value_up, 'ctx', axis=1, tiled=True)  32.7 us
    all_gather x1, waiting for transfers between devices, per_device(): lax.all_gather(key_latent, 'ctx', axis=1, tiled=True)  29.1 us
    all_gather x1, blocking collectives, per_device(): lax.all_gather(key_rotary, 'ctx', axis=1, tiled=True)  24.5 us
    reduce_scatter x1, waiting for transfers between devices, per_device(): lax.psum_scatter(jnp.dot(heads_out, flat_out, preferred_element_type=jnp....  24.1 us
    all_to_all x1, starting transfers between devices, per_device(): lax.all_to_all(outgoing, ('ctx', 'tp'), split_axis=0, concat_axis=0, tile...  12.2 us
  transfers between devices with their start and end apart: 9, of which 6 were waited for; matrix products, arithmetic and copies ran while one was open for 11% of the time, Pallas kernels for 0%

commit v1 on v0

--- a/solution.py
+++ b/solution.py
@@ -5,6 +5,28 @@
 
 route_scale = 2.5
 norm_eps = 1e-06
+
+
+def in_order(blocks, dim):
+    blocks = jnp.moveaxis(blocks, 0, dim)
+    dims = blocks.shape
+    return blocks.reshape(*dims[:dim], dims[dim] * dims[dim + 1], *dims[dim + 2 :])
+
+
+def ring_gather(x, axis, dim):
+    peers = lax.axis_size(axis)
+    pairs = [(i, (i + 1) % peers) for i in range(peers)]
+    back = [(b, a) for a, b in pairs]
+    lower, upper = ([], [])
+    for step in range(peers - 1):
+        if step % 2 == 0:
+            lower.append(lax.ppermute(lower[-1] if lower else x, axis, pairs))
+        else:
+            upper.append(lax.ppermute(upper[-1] if upper else x, axis, back))
+    parts = jnp.stack([*lower[::-1], x, *upper])
+    shift = lax.axis_index(axis) - len(lower)
+    parts = parts[(jnp.arange(peers) - shift) % peers]
+    return in_order(parts, dim)
 
 
 def rms_scale(rows_in, norm_gain):
@@ -71,7 +93,7 @@
         jnp.zeros((head_count, rows_here, latent_width), jnp.float32),
     )
     pieces = (
-        lax.all_gather(key_latent, "ctx", axis=1, tiled=True),
+        ring_gather(key_latent, "ctx", 1),
         lax.all_gather(key_rotary, "ctx", axis=1, tiled=True),
     )
 

time: 530 us -> 485 us (0.915)
  waiting for transfers between devices: 325 us -> 232 us
  starting transfers between devices: 31.9 us -> 59.2 us
  local copies, waits for them, and re-layouts: 41.3 us -> 58 us
    all_gather x1, waiting for transfers between devices: 73.1 us -> 7.3 us  [per_device(): lax.all_gather(out_proj, 'ctx', axis=2, tiled=True)]
    ppermute x0 -> x15, starting transfers between devices: none -> 38.8 us  [the longest x7 37.3 us: ring_gather(): upper.append(lax.ppermute(upper[-1] if upper else x, axis, back))]
    all_gather x1, waiting for transfers between devices: 32.7 us -> 0.01 us  [per_device(): lax.all_gather(value_up, 'ctx', axis=1, tiled=True)]
    all_gather x1 -> x0, waiting for transfers between devices: 29.1 us -> none  [per_device(): lax.all_gather(key_latent, 'ctx', axis=1, tiled=True)]
    ppermute x0 -> x15, waiting for transfers between devices: none -> 23.1 us  [the longest x8 19.1 us: ring_gather(): lower.append(lax.ppermute(lower[-1] if lower else x, axis, pairs))]
    unnamed x24 -> x67, local copies, waits for them, and re-layouts: 7.29 us -> 23.1 us
    all_gather x1, starting transfers between devices: 11.6 us -> 0.04 us  [per_device(): lax.all_gather(up_proj, 'dp', axis=1, tiled=True)]
    reduce_scatter x1, waiting for transfers between devices: 24.1 us -> 35.1 us  [per_device(): lax.psum_scatter(jnp.dot(heads_out, flat_out, preferred_element_type=jnp....]
  transfers between devices with their start and end apart: 9 -> 23, of which waited for: 6 -> 15; matrix products, arithmetic and copies ran while one was open for 11% -> 15% of each run, Pallas kernels for 0% -> 0%
where the time goes in v1:
time: 485 us; the launch traced here: 475 us
  waiting for transfers between devices  232 us (48%)
  matrix products  69.3 us (14%)
  starting transfers between devices  59.2 us (12%)
  local copies, waits for them, and re-layouts  58 us (12%)
  blocking collectives  24.6 us (5%)
  between operations  16.3 us (3%)
  other arithmetic  15.9 us (3%)
    all_to_all x1, waiting for transfers between devices, per_device(): lax.all_to_all(outgoing, ('ctx', 'tp'), split_axis=0, concat_axis=0, tile...  82.5 us
    all_to_all x1, waiting for transfers between devices, per_device(): lax.all_to_all(going_back, ('ctx', 'tp'), split_axis=0, concat_axis=0, ti...  81 us
    ppermute x7, starting transfers between devices, ring_gather(): upper.append(lax.ppermute(upper[-1] if upper else x, axis, back))  37.3 us
    reduce_scatter x1, waiting for transfers between devices, per_device(): lax.psum_scatter(jnp.dot(heads_out, flat_out, preferred_element_type=jnp....  35.1 us
    all_gather x1, blocking collectives, per_device(): lax.all_gather(key_rotary, 'ctx', axis=1, tiled=True)  24.6 us
    unnamed x67, local copies, waits for them, and re-layouts  23.1 us
    ppermute x8, waiting for transfers between devices, ring_gather(): lower.append(lax.ppermute(lower[-1] if lower else x, axis, pairs))  19.1 us
    all_to_all x1, starting transfers between devices, per_device(): lax.all_to_all(outgoing, ('ctx', 'tp'), split_axis=0, concat_axis=0, tile...  12.1 us
  transfers between devices with their start and end apart: 23, of which 15 were waited for; matrix products, arithmetic and copies ran while one was open for 15% of the time, Pallas kernels for 0%

profile of v1, /device:TPU:32, one launch (start us, length us, event | category | flops | bytes accessed | tf_op | source)
XLA Modules:
  0.0 475.2 jit_solution(15049560043492144436)
XLA Ops:
  9.5 1.6 collective-permute-start
  11.1 7.4 %collective-permute-done = bf16[1,128,512]{2,1,0:T(8,128)(2,1)S(1)} collective-permute-done((bf16[1,128,512]{2,1,0:T(8,128)(2,1)}, bf16[1,128,512]{2,1,0:T(8,128)(2,1)S(1)}, u32[]{:S(2)}, u32[]{:S(2)}) %collective-permute-start) | collective-permute-done | bytes 131104 | tf_op jit(solution)/shard_map/ppermute | solution.py:23
  19.2 5.3 %collective-permute-start.8 = (bf16[1,128,512]{2,1,0:T(8,128)(2,1)}, bf16[1,128,512]{2,1,0:T(8,128)(2,1)S(1)}, u32[]{:S(2)}, u32[]{:S(2)}) collective-permute-start(bf16[1,128,512]{2,1,0:T(8,128)(2,1)} %param.18), channel_id=1, source_target_pairs={{16,0},{32,16},{48,32},{64,48},{80,64},{96,80},{112,96},{128,112},... | collective-permute-start | bytes 393224 | tf_op jit(solution)/shard_map/ppermute | solution.py:25
  24.5 2.9 collective-permute-done.1
  28.2 5.7 %collective-permute-start.9 = (bf16[1,128,512]{2,1,0:T(8,128)(2,1)S(1)}, bf16[1,128,512]{2,1,0:T(8,128)(2,1)S(1)}, u32[]{:S(2)}, u32[]{:S(2)}) collective-permute-start(bf16[1,128,512]{2,1,0:T(8,128)(2,1)S(1)} %collective-permute-done.8), channel_id=1, source_target_pairs={{16,0},{32,16},{48,32},{64,48},{80,64},{96,80},{112,96},{128,112},... | collective-permute-start | bytes 393224 | tf_op jit(solution)/shard_map/ppermute | solution.py:25
  33.9 2.2 collective-permute-done.2
  36.6 5.9 %collective-permute-start.10 = (bf16[1,128,512]{2,1,0:T(8,128)(2,1)S(1)}, bf16[1,128,512]{2,1,0:T(8,128)(2,1)S(1)}, u32[]{:S(2)}, u32[]{:S(2)}) collective-permute-start(bf16[1,128,512]{2,1,0:T(8,128)(2,1)S(1)} %collective-permute-done.9), channel_id=1, source_target_pairs={{16,0},{32,16},{48,32},{64,48},{80,64},{96,80},{112,96},{128,112},... | collective-permute-start | bytes 393224 | tf_op jit(solution)/shard_map/ppermute | solution.py:25
  42.5 1.9 collective-permute-done.3
  45.0 5.8 %collective-permute-start.11 = (bf16[1,128,512]{2,1,0:T(8,128)(2,1)S(1)}, bf16[1,128,512]{2,1,0:T(8,128)(2,1)S(1)}, u32[]{:S(2)}, u32[]{:S(2)}) collective-permute-start(bf16[1,128,512]{2,1,0:T(8,128)(2,1)S(1)} %collective-permute-done.10), channel_id=1, source_target_pairs={{16,0},{32,16},{48,32},{64,48},{80,64},{96,80},{112,96},{128,112},... | collective-permute-start | bytes 393224 | tf_op jit(solution)/shard_map/ppermute | solution.py:25
  50.8 2.0 collective-permute-done.4
  53.9 5.8 %collective-permute-start.12 = (bf16[1,128,512]{2,1,0:T(8,128)(2,1)S(1)}, bf16[1,128,512]{2,1,0:T(8,128)(2,1)S(1)}, u32[]{:S(2)}, u32[]{:S(2)}) collective-permute-start(bf16[1,128,512]{2,1,0:T(8,128)(2,1)S(1)} %collective-permute-done.11), channel_id=1, source_target_pairs={{16,0},{32,16},{48,32},{64,48},{80,64},{96,80},{112,96},{128,112},... | collective-permute-start | bytes 393224 | tf_op jit(solution)/shard_map/ppermute | solution.py:25
  59.7 1.4 collective-permute-done.5
  61.1 2.4 collective-permute-done.12
  63.6 5.9 %collective-permute-start.13 = (bf16[1,128,512]{2,1,0:T(8,128)(2,1)S(1)}, bf16[1,128,512]{2,1,0:T(8,128)(2,1)}, u32[]{:S(2)}, u32[]{:S(2)}) collective-permute-start(bf16[1,128,512]{2,1,0:T(8,128)(2,1)S(1)} %collective-permute-done.12), channel_id=1, source_target_pairs={{16,0},{32,16},{48,32},{64,48},{80,64},{96,80},{112,96},{128,112},... | collective-permute-start | bytes 393224 | tf_op jit(solution)/shard_map/ppermute | solution.py:25
  70.6 24.6 %all_gather.18 = bf16[1,2048,64]{1,2,0:T(8,128)(2,1)S(1)} all-gather(bf16[1,128,64]{1,2,0:T(8,128)(2,1)} %param.19), channel_id=1, replica_groups=mesh['ctx'=16,'tp'=8,'dp'=2] {'ctx'}, dimensions={1}, use_global_device_ids=true | all-gather | bytes 278528 | tf_op jit(solution)/shard_map/all_gather | solution.py:97
  95.2 2.9 collective-permute-start.14
  112.1 19.9 %conditional.1 = (f32[8,128]{1,0:T(8,128)S(1)}, f32[8,128,512]{2,1,0:T(8,128)}) conditional(s32[]{:T(128)} %convert_element_type.71, () %tuple.28, (s32[]{:T(128)}, s32[128]{0:T(128)S(1)}, s32[16,1]{0,1:T(1,128)S(1)}, s32[]{:T(128)}, s32[]{:T(128)}, /*index=5*/bf16[16,1,128,512]{3,2,1,0:T(8,128)(2,1)S(1)}, ...), branch_computations={%region_0.1_spmd, %region_1.4_spmd.clone.clone} | conditional | flops 4584636928 | bytes 65697604 | solution.py:123
  112.1 2.0 gather_fusion
  114.5 6.5 %fusion.7 = f32[2048,128,8]{1,0,2:T(8,128)} fusion(bf16[2048,512,1]{1,0,2:T(8,128)(2,1)} %bitcast.176, bf16[128,8,512]{2,1,0:T(8,128)(2,1)S(1)} %bitcast.179), kind=kOutput, calls=%fused_computation.9 | convolution fusion | flops 2147483648 | bytes 11534336 | tf_op jit(solution)/shard_map/cond/branch_1_fun/qhc,kc->hqk/dot_general | solution.py:105
  121.4 5.2 %fusion.69 = (f32[8,128]{1,0:T(8,128)S(1)}, f32[8,128,2048]{1,2,0:T(8,128)S(1)}) fusion(f32[2048,128,8]{1,0,2:T(8,128)} %fusion.7, bf16[128,8,64]{0,2,1:T(8,128)(2,1)S(1)} %bitcast.180, bf16[1,2048,64]{1,2,0:T(8,128)(2,1)S(1)} %get-tuple-element.200, pred[128,2048]{0,1:T(8,128)(4,1)S(1)} %iota_compare_fusion), kind=kOutput, calls=%fused_computation.117 | convolution fusion | flops 276823040 | bytes 17436672 | tf_op jit(solution)/shard_map/cond/branch_1_fun/qhr,kr->hqk/dot_general | solution.py:106
  126.6 1.4 fusion.1
  128.2 3.7 fusion.2
  132.0 7.3 %all-gather.8.cloned.1.call-done = bf16[8,128,3584]{1,2,0:T(8,128)(2,1)} async-done(((bf16[8,128,224]{1,2,0:T(8,128)(2,1)}), bf16[8,128,3584]{1,2,0:T(8,128)(2,1)}) %all-gather.8.cloned.1.call-update) | async-done | bytes 7340048 | tf_op jit(solution)/shard_map/all_gather | solution.py:130
  139.3 7.8 %fusion.34 = bf16[128,3584]{1,0:T(8,128)(2,1)} fusion(bf16[8,128,3584]{1,2,0:T(8,128)(2,1)} %all-gather.8.cloned.1.call-done, bf16[8,512,128]{2,1,0:T(8,128)(2,1)} %all-gather.6.cloned.1.call-done, f32[8,128,512]{2,1,0:T(8,128)} %get-tuple-element.136, f32[8,128]{1,0:T(8,128)S(1)} %get-tuple-element.137), kind=kOutput, calls=%fused_computation.40 | convolution fusion | flops 1075380224 | bytes 11407360 | tf_op jit(solution)/shard_map/dot_general | solution.py:135
  149.4 35.1 %reduce-scatter.2.cloned.1.call-done = bf16[16,3584]{1,0:T(8,128)(2,1)} async-done(((bf16[128,3584]{1,0:T(8,128)(2,1)}), bf16[16,3584]{1,0:T(8,128)(2,1)}) %reduce-scatter.2.cloned.1.call-update) | async-done | bytes 114704 | tf_op jit(solution)/shard_map/reduce_scatter | solution.py:134
  186.6 3.0 convolution_convert_fusion
  189.6 9.5 %reshape.152 = bf16[128,2,2,3584]{3,2,1,0:T(2,128)(2,1)} reshape(bf16[256,7168]{1,0:T(8,128)(2,1)} %convolution_convert_fusion) | data formatting | bytes 7340032 | tf_op jit(solution)/shard_map/reshape | solution.py:157
  199.0 12.1 %all-to-all-start = ((bf16[128,2,2,3584]{3,2,1,0:T(2,128)(2,1)}), bf16[128,2,2,3584]{3,2,1,0:T(2,128)(2,1)}, u32[]{:S(2)}, u32[]{:S(2)}) async-start(bf16[128,2,2,3584]{3,2,1,0:T(2,128)(2,1)} %reshape.152), calls=%async_computation.1 | async-start | bytes 7340032 | tf_op jit(solution)/shard_map/all_to_all | solution.py:166
  211.7 82.5 %all-to-all-done = bf16[128,2,2,3584]{3,2,1,0:T(2,128)(2,1)} async-done(((bf16[128,2,2,3584]{3,2,1,0:T(2,128)(2,1)}), bf16[128,2,2,3584]{3,2,1,0:T(2,128)(2,1)}, u32[]{:S(2)}, u32[]{:S(2)}) %all-to-all-start) | async-done | bytes 3670048 | tf_op jit(solution)/shard_map/all_to_all | solution.py:166
  294.2 8.9 %fusion.70 = (bf16[256,1,3584]{2,1,0:T(2,128)(2,1)}, bf16[256,1,3584]{2,1,0:T(2,128)(2,1)}) fusion(bf16[256,2,3584]{2,1,0:T(2,128)(2,1)} %bitcast.26), kind=kLoop, calls=%fused_computation.118 | loop fusion | bytes 7340032 | tf_op jit(solution)/shard_map/slice | solution.py:170
  303.1 6.3 %fusion.23 = f32[256,1024]{1,0:T(8,128)S(1)} fusion(bf16[1,3584,1024]{2,1,0:T(8,128)(2,1)} %all-gather.10.cloned.1.call-done, bf16[256,1,3584]{2,1,0:T(2,128)(2,1)} %get-tuple-element.215), kind=kOutput, calls=%fused_computation.34 | convolution fusion | flops 1879048192 | bytes 10223616 | tf_op jit(solution)/shard_map/dot_general | solution.py:38
  309.4 7.3 %fusion.19 = f32[256,1024]{1,0:T(8,128)} fusion(bf16[1,3584,1024]{2,1,0:T(8,128)(2,1)} %all-gather.12.cloned.1.call-done, bf16[256,1,3584]{2,1,0:T(2,128)(2,1)} %get-tuple-element.215), kind=kOutput, calls=%fused_computation.30 | convolution fusion | flops 1879048192 | bytes 10223616 | tf_op jit(solution)/shard_map/dot_general | solution.py:39
  316.7 6.4 %fusion.13 = f32[256,1024]{1,0:T(8,128)S(1)} fusion(bf16[1,1024,3584]{2,1,0:T(8,128)(2,1)} %all-gather.14.cloned.1.call-done, bf16[256,1,3584]{2,1,0:T(2,128)(2,1)} %get-tuple-element.216), kind=kOutput, calls=%fused_computation.24 | convolution fusion | flops 1879048192 | bytes 10223616 | tf_op jit(solution)/shard_map/dot_general | solution.py:43
  324.1 2.2 fusion.17
  326.3 3.9 fusion.31
  330.2 3.7 stack.81
  333.9 5.5 %fusion.28 = bf16[256,3584]{1,0:T(8,128)(2,1)S(1)} fusion(bf16[1,1024,3584]{2,1,0:T(8,128)(2,1)} %all-gather.14.cloned.1.call-done, f32[256,1024]{1,0:T(8,128)} %fusion.19, f32[256,1024]{1,0:T(8,128)S(1)} %fusion.23), kind=kOutput, calls=%fused_computation.37 | convolution fusion | flops 1881538560 | bytes 11272192 | tf_op jit(solution)/shard_map/dot_general | solution.py:42
  339.4 3.8 stack.80
  343.2 10.0 %pad_maximum_fusion = bf16[128,2,2,3584]{3,2,1,0:T(2,128)(2,1)} fusion(bf16[128,2,1,3584]{3,2,1,0:T(2,128)(2,1)} %stack.81, bf16[128,2,1,3584]{3,2,1,0:T(2,128)(2,1)} %stack.80), kind=kLoop, calls=%fused_computation.41 | loop fusion | flops 7340032 | bytes 7340032 | tf_op jit(solution)/shard_map/stack | solution.py:171
  353.3 7.8 %all-to-all-start.1 = ((bf16[128,2,2,3584]{3,2,1,0:T(2,128)(2,1)}), bf16[128,2,2,3584]{3,2,1,0:T(2,128)(2,1)}, u32[]{:S(2)}, u32[]{:S(2)}) async-start(bf16[128,2,2,3584]{3,2,1,0:T(2,128)(2,1)} %pad_maximum_fusion), calls=%async_computation.2 | async-start | bytes 7340032 | tf_op jit(solution)/shard_map/all_to_all | solution.py:172
  361.1 81.0 %all-to-all-done.1 = bf16[128,2,2,3584]{3,2,1,0:T(2,128)(2,1)} async-done(((bf16[128,2,2,3584]{3,2,1,0:T(2,128)(2,1)}), bf16[128,2,2,3584]{3,2,1,0:T(2,128)(2,1)}, u32[]{:S(2)}, u32[]{:S(2)}) %all-to-all-start.1) | async-done | bytes 3670048 | tf_op jit(solution)/shard_map/all_to_all | solution.py:172
  442.1 4.4 copy.63
  446.5 5.9 %copy.49 = bf16[7168,256]{1,0:T(8,128)(2,1)} copy(bf16[7168,256]{0,1:T(8,128)(2,1)} %bitcast.173) | data formatting | bytes 7340032 | tf_op jit(solution)/shard_map/dot_general | solution.py:173
  452.4 3.4 fusion.51
  455.8 1.8 copy-done
  457.5 1.9 fusion.36
  459.7 3.1 fusion.35
  462.7 3.1 fusion.37
  (130 shorter events, 28.5 us)
Async XLA Ops:
  8.0 104.1 %copy-start.4 = (bf16[1,128,4096]{2,1,0:T(8,128)(2,1)S(1)}, bf16[1,128,4096]{2,1,0:T(8,128)(2,1)}, u32[]{:S(2)}) copy-start(bf16[1,128,4096]{2,1,0:T(8,128)(2,1)} %param.16) | copy-start | bytes 3145732
  8.0 104.1 %copy-start.7 = (bf16[1,128,512]{2,1,0:T(8,128)(2,1)S(1)}, bf16[1,128,512]{2,1,0:T(8,128)(2,1)}, u32[]{:S(2)}) copy-start(bf16[1,128,512]{2,1,0:T(8,128)(2,1)} %param.17) | copy-start | bytes 393220
  8.0 124.0 %all-gather.6.cloned.1.call-start = ((), (), s32[]{:S(2)}) async-start(), calls=%async_computation.3 | async-start | bytes 1114112 | tf_op jit(solution)/shard_map/all_gather | solution.py:129
  8.8 130.5 %all-gather.8.cloned.1.call-start = ((), (), s32[]{:S(2)}) async-start(), calls=%async_computation.4 | async-start | bytes 7798784 | tf_op jit(solution)/shard_map/all_gather | solution.py:130
  9.5 175.0 %reduce-scatter.2.cloned.1.call-start = ((), (), s32[]{:S(2)}) async-start(), calls=%async_computation.5 | async-start | bytes 1032192 | tf_op jit(solution)/shard_map/reduce_scatter | solution.py:134
  9.5 9.0 %collective-permute-start = (bf16[1,128,512]{2,1,0:T(8,128)(2,1)}, bf16[1,128,512]{2,1,0:T(8,128)(2,1)S(1)}, u32[]{:S(2)}, u32[]{:S(2)}) collective-permute-start(bf16[1,128,512]{2,1,0:T(8,128)(2,1)} %param.18), channel_id=1, source_target_pairs={{0,16},{16,32},{32,48},{48,64},{64,80},{80,96},{96,112},{112,128},... | collective-permute-start | bytes 393224 | tf_op jit(solution)/shard_map/ppermute | solution.py:23
  19.2 8.3 %collective-permute-start.1 = (bf16[1,128,512]{2,1,0:T(8,128)(2,1)S(1)}, bf16[1,128,512]{2,1,0:T(8,128)(2,1)S(1)}, u32[]{:S(2)}, u32[]{:S(2)}) collective-permute-start(bf16[1,128,512]{2,1,0:T(8,128)(2,1)S(1)} %collective-permute-done), channel_id=1, source_target_pairs={{0,16},{16,32},{32,48},{48,64},{64,80},{80,96},{96,112},{112,128},... | collective-permute-start | bytes 393224 | tf_op jit(solution)/shard_map/ppermute | solution.py:23
  19.2 8.3 %collective-permute-start.8 = (bf16[1,128,512]{2,1,0:T(8,128)(2,1)}, bf16[1,128,512]{2,1,0:T(8,128)(2,1)S(1)}, u32[]{:S(2)}, u32[]{:S(2)}) collective-permute-start(bf16[1,128,512]{2,1,0:T(8,128)(2,1)} %param.18), channel_id=1, source_target_pairs={{16,0},{32,16},{48,32},{64,48},{80,64},{96,80},{112,96},{128,112},... | collective-permute-start | bytes 393224 | tf_op jit(solution)/shard_map/ppermute | solution.py:25
  27.5 9.1 %copy-start.10 = (bf16[1,128,512]{2,1,0:T(8,128)(2,1)}, bf16[1,128,512]{2,1,0:T(8,128)(2,1)S(1)}, u32[]{:S(2)}) copy-start(bf16[1,128,512]{2,1,0:T(8,128)(2,1)S(1)} %collective-permute-done.1) | copy-start | bytes 393220
  27.5 8.6 %collective-permute-start.2 = (bf16[1,128,512]{2,1,0:T(8,128)(2,1)S(1)}, bf16[1,128,512]{2,1,0:T(8,128)(2,1)S(1)}, u32[]{:S(2)}, u32[]{:S(2)}) collective-permute-start(bf16[1,128,512]{2,1,0:T(8,128)(2,1)S(1)} %collective-permute-done.1), channel_id=1, source_target_pairs={{0,16},{16,32},{32,48},{48,64},{64,80},{80,96},{96,112},{112,128},... | collective-permute-start | bytes 393224 | tf_op jit(solution)/shard_map/ppermute | solution.py:23
  27.5 0.7 copy-start.9
  28.2 8.4 %collective-permute-start.9 = (bf16[1,128,512]{2,1,0:T(8,128)(2,1)S(1)}, bf16[1,128,512]{2,1,0:T(8,128)(2,1)S(1)}, u32[]{:S(2)}, u32[]{:S(2)}) collective-permute-start(bf16[1,128,512]{2,1,0:T(8,128)(2,1)S(1)} %collective-permute-done.8), channel_id=1, source_target_pairs={{16,0},{32,16},{48,32},{64,48},{80,64},{96,80},{112,96},{128,112},... | collective-permute-start | bytes 393224 | tf_op jit(solution)/shard_map/ppermute | solution.py:25
  36.1 8.9 %copy-start.12 = (bf16[1,128,512]{2,1,0:T(8,128)(2,1)}, bf16[1,128,512]{2,1,0:T(8,128)(2,1)S(1)}, u32[]{:S(2)}) copy-start(bf16[1,128,512]{2,1,0:T(8,128)(2,1)S(1)} %collective-permute-done.2) | copy-start | bytes 393220
  36.1 8.3 %collective-permute-start.3 = (bf16[1,128,512]{2,1,0:T(8,128)(2,1)S(1)}, bf16[1,128,512]{2,1,0:T(8,128)(2,1)S(1)}, u32[]{:S(2)}, u32[]{:S(2)}) collective-permute-start(bf16[1,128,512]{2,1,0:T(8,128)(2,1)S(1)} %collective-permute-done.2), channel_id=1, source_target_pairs={{0,16},{16,32},{32,48},{48,64},{64,80},{80,96},{96,112},{112,128},... | collective-permute-start | bytes 393224 | tf_op jit(solution)/shard_map/ppermute | solution.py:23
  36.6 5.9 %copy-start.11 = (bf16[1,128,512]{2,1,0:T(8,128)(2,1)}, bf16[1,128,512]{2,1,0:T(8,128)(2,1)S(1)}, u32[]{:S(2)}) copy-start(bf16[1,128,512]{2,1,0:T(8,128)(2,1)S(1)} %collective-permute-done.9) | copy-start | bytes 393220
  36.6 8.4 %collective-permute-start.10 = (bf16[1,128,512]{2,1,0:T(8,128)(2,1)S(1)}, bf16[1,128,512]{2,1,0:T(8,128)(2,1)S(1)}, u32[]{:S(2)}, u32[]{:S(2)}) collective-permute-start(bf16[1,128,512]{2,1,0:T(8,128)(2,1)S(1)} %collective-permute-done.9), channel_id=1, source_target_pairs={{16,0},{32,16},{48,32},{64,48},{80,64},{96,80},{112,96},{128,112},... | collective-permute-start | bytes 393224 | tf_op jit(solution)/shard_map/ppermute | solution.py:25
  44.4 19.2 %copy-start.15 = (bf16[1,128,512]{2,1,0:T(8,128)(2,1)}, bf16[1,128,512]{2,1,0:T(8,128)(2,1)S(1)}, u32[]{:S(2)}) copy-start(bf16[1,128,512]{2,1,0:T(8,128)(2,1)S(1)} %collective-permute-done.3) | copy-start | bytes 393220
  44.4 8.4 %collective-permute-start.4 = (bf16[1,128,512]{2,1,0:T(8,128)(2,1)S(1)}, bf16[1,128,512]{2,1,0:T(8,128)(2,1)S(1)}, u32[]{:S(2)}, u32[]{:S(2)}) collective-permute-start(bf16[1,128,512]{2,1,0:T(8,128)(2,1)S(1)} %collective-permute-done.3), channel_id=1, source_target_pairs={{0,16},{16,32},{32,48},{48,64},{64,80},{80,96},{96,112},{112,128},... | collective-permute-start | bytes 393224 | tf_op jit(solution)/shard_map/ppermute | solution.py:23
  45.0 5.8 %copy-start.13 = (bf16[1,128,512]{2,1,0:T(8,128)(2,1)}, bf16[1,128,512]{2,1,0:T(8,128)(2,1)S(1)}, u32[]{:S(2)}) copy-start(bf16[1,128,512]{2,1,0:T(8,128)(2,1)S(1)} %collective-permute-done.10) | copy-start | bytes 393220
  45.0 8.3 %collective-permute-start.11 = (bf16[1,128,512]{2,1,0:T(8,128)(2,1)S(1)}, bf16[1,128,512]{2,1,0:T(8,128)(2,1)S(1)}, u32[]{:S(2)}, u32[]{:S(2)}) collective-permute-start(bf16[1,128,512]{2,1,0:T(8,128)(2,1)S(1)} %collective-permute-done.10), channel_id=1, source_target_pairs={{16,0},{32,16},{48,32},{64,48},{80,64},{96,80},{112,96},{128,112},... | collective-permute-start | bytes 393224 | tf_op jit(solution)/shard_map/ppermute | solution.py:25
  52.8 16.7 %copy-start.17 = (bf16[1,128,512]{2,1,0:T(8,128)(2,1)}, bf16[1,128,512]{2,1,0:T(8,128)(2,1)S(1)}, u32[]{:S(2)}) copy-start(bf16[1,128,512]{2,1,0:T(8,128)(2,1)S(1)} %collective-permute-done.4) | copy-start | bytes 393220
  52.8 8.4 %collective-permute-start.5 = (bf16[1,128,512]{2,1,0:T(8,128)(2,1)S(1)}, bf16[1,128,512]{2,1,0:T(8,128)(2,1)S(1)}, u32[]{:S(2)}, u32[]{:S(2)}) collective-permute-start(bf16[1,128,512]{2,1,0:T(8,128)(2,1)S(1)} %collective-permute-done.4), channel_id=1, source_target_pairs={{0,16},{16,32},{32,48},{48,64},{64,80},{80,96},{96,112},{112,128},... | collective-permute-start | bytes 393224 | tf_op jit(solution)/shard_map/ppermute | solution.py:23
  53.3 0.7 copy-start.14
  53.9 9.6 %collective-permute-start.12 = (bf16[1,128,512]{2,1,0:T(8,128)(2,1)S(1)}, bf16[1,128,512]{2,1,0:T(8,128)(2,1)S(1)}, u32[]{:S(2)}, u32[]{:S(2)}) collective-permute-start(bf16[1,128,512]{2,1,0:T(8,128)(2,1)S(1)} %collective-permute-done.11), channel_id=1, source_target_pairs={{16,0},{32,16},{48,32},{64,48},{80,64},{96,80},{112,96},{128,112},... | collective-permute-start | bytes 393224 | tf_op jit(solution)/shard_map/ppermute | solution.py:25
  61.1 9.5 %copy-start.18 = (bf16[1,128,512]{2,1,0:T(8,128)(2,1)}, bf16[1,128,512]{2,1,0:T(8,128)(2,1)S(1)}, u32[]{:S(2)}) copy-start(bf16[1,128,512]{2,1,0:T(8,128)(2,1)S(1)} %collective-permute-done.5) | copy-start | bytes 393220
  61.1 9.5 %collective-permute-start.6 = (bf16[1,128,512]{2,1,0:T(8,128)(2,1)S(1)}, bf16[1,128,512]{2,1,0:T(8,128)(2,1)S(1)}, u32[]{:S(2)}, u32[]{:S(2)}) collective-permute-start(bf16[1,128,512]{2,1,0:T(8,128)(2,1)S(1)} %collective-permute-done.5), channel_id=1, source_target_pairs={{0,16},{16,32},{32,48},{48,64},{64,80},{80,96},{96,112},{112,128},... | collective-permute-start | bytes 393224 | tf_op jit(solution)/shard_map/ppermute | solution.py:23
  63.6 34.6 %copy-start.16 = (bf16[1,128,512]{2,1,0:T(8,128)(2,1)}, bf16[1,128,512]{2,1,0:T(8,128)(2,1)S(1)}, u32[]{:S(2)}) copy-start(bf16[1,128,512]{2,1,0:T(8,128)(2,1)S(1)} %collective-permute-done.12) | copy-start | bytes 393220
  63.6 31.7 %collective-permute-start.13 = (bf16[1,128,512]{2,1,0:T(8,128)(2,1)S(1)}, bf16[1,128,512]{2,1,0:T(8,128)(2,1)}, u32[]{:S(2)}, u32[]{:S(2)}) collective-permute-start(bf16[1,128,512]{2,1,0:T(8,128)(2,1)S(1)} %collective-permute-done.12), channel_id=1, source_target_pairs={{16,0},{32,16},{48,32},{64,48},{80,64},{96,80},{112,96},{128,112},... | collective-permute-start | bytes 393224 | tf_op jit(solution)/shard_map/ppermute | solution.py:25
  70.6 27.6 %copy-start.19 = (bf16[1,128,512]{2,1,0:T(8,128)(2,1)}, bf16[1,128,512]{2,1,0:T(8,128)(2,1)S(1)}, u32[]{:S(2)}) copy-start(bf16[1,128,512]{2,1,0:T(8,128)(2,1)S(1)} %collective-permute-done.6) | copy-start | bytes 393220
  70.6 27.6 %collective-permute-start.7 = (bf16[1,128,512]{2,1,0:T(8,128)(2,1)S(1)}, bf16[1,128,512]{2,1,0:T(8,128)(2,1)}, u32[]{:S(2)}, u32[]{:S(2)}) collective-permute-start(bf16[1,128,512]{2,1,0:T(8,128)(2,1)S(1)} %collective-permute-done.6), channel_id=1, source_target_pairs={{0,16},{16,32},{32,48},{48,64},{64,80},{80,96},{96,112},{112,128},... | collective-permute-start | bytes 393224 | tf_op jit(solution)/shard_map/ppermute | solution.py:23
  95.2 16.8 %collective-permute-start.14 = (bf16[1,128,512]{2,1,0:T(8,128)(2,1)}, bf16[1,128,512]{2,1,0:T(8,128)(2,1)S(1)}, u32[]{:S(2)}, u32[]{:S(2)}) collective-permute-start(bf16[1,128,512]{2,1,0:T(8,128)(2,1)} %collective-permute-done.13), channel_id=1, source_target_pairs={{16,0},{32,16},{48,32},{64,48},{80,64},{96,80},{112,96},{128,112},... | collective-permute-start | bytes 393224 | tf_op jit(solution)/shard_map/ppermute | solution.py:25
  126.6 1.6 copy-start.1
  147.1 1.2 copy-start.20
  147.2 37.3 %copy-start.2 = (bf16[1,16,3584]{2,1,0:T(8,128)(2,1)S(1)}, bf16[1,16,3584]{2,1,0:T(8,128)(2,1)}, u32[]{:S(2)}) copy-start(bf16[1,16,3584]{2,1,0:T(8,128)(2,1)} %param.22) | copy-start | bytes 344068
  147.2 38.4 %copy-start.6 = (f32[3584]{0:T(1024)S(1)}, f32[3584]{0:T(1024)}, u32[]{:S(2)}) copy-start(f32[3584]{0:T(1024)} %param.23) | copy-start | bytes 43012
  147.2 39.4 %copy-start.5 = (bf16[1,16,3584]{2,1,0:T(8,128)(2,1)S(1)}, bf16[1,16,3584]{2,1,0:T(8,128)(2,1)}, u32[]{:S(2)}) copy-start(bf16[1,16,3584]{2,1,0:T(8,128)(2,1)} %param.29) | copy-start | bytes 344068
  147.2 155.9 %all-gather.10.cloned.1.call-start = ((), (), s32[]{:S(2)}) async-start(), calls=%async_computation.6 | async-start | bytes 11010048 | tf_op jit(solution)/shard_map/all_gather | solution.py:159
  147.8 161.6 %all-gather.12.cloned.1.call-start = ((), (), s32[]{:S(2)}) async-start(), calls=%async_computation.7 | async-start | bytes 11010048 | tf_op jit(solution)/shard_map/all_gather | solution.py:160
  199.0 95.2 %all-to-all-start = ((bf16[128,2,2,3584]{3,2,1,0:T(2,128)(2,1)}), bf16[128,2,2,3584]{3,2,1,0:T(2,128)(2,1)}, u32[]{:S(2)}, u32[]{:S(2)}) async-start(bf16[128,2,2,3584]{3,2,1,0:T(2,128)(2,1)} %reshape.152), calls=%async_computation.1 | async-start | bytes 7340032 | tf_op jit(solution)/shard_map/all_to_all | solution.py:166
  211.2 105.5 %all-gather.14.cloned.1.call-start = ((), (), s32[]{:S(2)}) async-start(), calls=%async_computation.8 | async-start | bytes 11010048 | tf_op jit(solution)/shard_map/all_gather | solution.py:161
  316.7 7.4 %copy-start.22 = (bf16[1,3584,1024]{2,1,0:T(8,128)(2,1)S(1)}, bf16[1,3584,1024]{2,1,0:T(8,128)(2,1)}, u32[]{:S(2)}) copy-start(bf16[1,3584,1024]{2,1,0:T(8,128)(2,1)} %all-gather.12.cloned.1.call-done) | copy-start | bytes 22020100
  316.7 9.6 %slice-start = ((s8[7340032]{0:T(1024)(128)(4,1)}), s8[4194304]{0:T(1024)(128)(4,1)S(1)}, s32[]{:S(2)}) async-start(s8[7340032]{0:T(1024)(128)(4,1)} %bitcast.183), calls=%async_computation.9 | async-start | bytes 8388608
  323.1 1.0 copy-start.23
  324.1 2.2 slice-start.1
  353.3 7.8 %copy-start.21 = (f32[1,16,8]{1,2,0:T(8,128)S(1)}, f32[1,16,8]{1,2,0:T(8,128)}, u32[]{:S(2)}) copy-start(f32[1,16,8]{1,2,0:T(8,128)} %param.28) | copy-start | bytes 1540
  353.3 88.8 %all-to-all-start.1 = ((bf16[128,2,2,3584]{3,2,1,0:T(2,128)(2,1)}), bf16[128,2,2,3584]{3,2,1,0:T(2,128)(2,1)}, u32[]{:S(2)}, u32[]{:S(2)}) async-start(bf16[128,2,2,3584]{3,2,1,0:T(2,128)(2,1)} %pad_maximum_fusion), calls=%async_computation.2 | async-start | bytes 7340032 | tf_op jit(solution)/shard_map/all_to_all | solution.py:172
  455.7 1.8 copy-start
  455.8 10.1 %copy-start.3 = (bf16[16,3584]{1,0:T(8,128)(2,1)S(1)}, bf16[16,3584]{1,0:T(8,128)(2,1)}, u32[]{:S(2)}) copy-start(bf16[16,3584]{1,0:T(8,128)(2,1)} %reduce-scatter.2.cloned.1.call-done) | copy-start | bytes 344068
  (1 other events, 0.6 us)
Sparse Core Ops, SparseCore 0:
  11.3 54.2 all-gather.5
  68.0 71.2 all-gather.7
  147.3 37.1 reduce-scatter.1
Sparse Core Ops, SparseCore 1:
  149.6 23.3 all-gather.9
  174.7 24.8 all-gather.11
  213.6 24.9 all-gather.13
